TPU v7x, 256 devices: a whole 4x4x8 slice. The times are simulated.
256 devices in a mesh: client: 32 (over z_lo, y, core), mp: 8 (over x, z_hi).
Axes of the slice: x: 4, y: 4, z: 8 (z_hi: 2, z_lo: 4; z = z_hi * 4 + z_lo), core: 2. Of those that a mesh axis runs over, the one named last changes fastest.
Arguments:
- hidden: bfloat16 [32, 4, 128, 7168], P('client', None, None, 'mp'), may hold values from -6 to 6
- weight: bfloat16 [32, 7168, 2048], P('client', 'mp'), may hold values from -0.0625 to 0.0625
- target: bfloat16 [32, 4, 128, 2048], P('client', None, 'mp'), may hold values from -6 to 6
- router_prob: float32 [32, 4, 128], P('client', None, 'mp'), may hold values from 0.2 to 1
- routes: int32 [32, 4, 128, 2], P('client', None, 'mp'), may hold values from 0 to 7, all different within a row
- assign: int32 [32, 1], replicated, may hold values from 0 to 3
Outputs:
- merged_weight: bfloat16 [32, 7168, 2048], P('client', 'mp')
Inputs may be any that keep to these rules, and one draw needn't show every extreme that they name: `routes`: each token names two different experts; the given weights are those of expert 0. `assign`: every cluster has at least one client.
All inputs are finite; a program needn't handle non-finite values.
Results may differ from a plain program's by a relative error of at most 0.0044.
The roundings to bfloat16 on the way count: a program that leaves them out, or rounds other values in their place, can miss the bound.
Values may be sent and summed in bfloat16 or wider, within the bound.
A program may use at most 128 MiB of HBM per device.

v0:
```python
import jax
import jax.numpy as jnp
from jax import lax
from jax.sharding import PartitionSpec as P

D = 2048
FFW = 7168
NB = 4
CLUSTERS = 4
EPS = 1e-06
FLOOR = 0.1


def body(hidden, weight, target, router_prob, routes, assign):
    local_weight = weight[0]
    fisher = jnp.zeros(local_weight.shape, jnp.float32)
    for batch in range(NB):
        batch_hidden = hidden[0, batch]
        outputs = lax.psum_scatter(
            jnp.dot(batch_hidden, local_weight, preferred_element_type=jnp.float32),
            "mp",
            scatter_dimension=0,
            tiled=True,
        )
        token_weight = jnp.where(
            jnp.any(routes[0, batch] == 0, axis=-1), router_prob[0, batch], 0.0
        )
        grad_out = (
            token_weight[:, None] * (outputs - target[0, batch].astype(jnp.float32))
        ).astype(jnp.bfloat16)
        grad = lax.dot_general(
            batch_hidden,
            lax.all_gather(grad_out, "mp", axis=0, tiled=True),
            (((0,), (0,)), ((), ())),
            preferred_element_type=jnp.float32,
        )
        fisher = fisher + grad * grad
    total_fisher = lax.psum(jnp.sum(fisher), "mp")
    mean_fisher = total_fisher / (FFW * D)
    a_weight = (fisher / (mean_fisher + EPS) + FLOOR).astype(jnp.bfloat16)
    got_a, got_w = (
        lax.all_to_all(a_weight[None], "client", split_axis=1, concat_axis=0, tiled=True),
        lax.all_to_all(local_weight[None], "client", split_axis=1, concat_axis=0, tiled=True),
    )
    member_table = (assign[:, 0][:, None] == jnp.arange(CLUSTERS)[None, :]).astype(jnp.float32)
    a_float = got_a.astype(jnp.float32)
    weighted = a_float * got_w.astype(jnp.float32)
    num_part = jnp.einsum("sk,srd->krd", member_table, weighted, precision=lax.Precision.HIGHEST)
    den_part = jnp.einsum("sk,srd->krd", member_table, a_float, precision=lax.Precision.HIGHEST)
    merged = (num_part / den_part).astype(jnp.bfloat16)
    own_cluster = lax.dynamic_index_in_dim(
        assign[:, 0], lax.axis_index("client"), 0, keepdims=False
    )
    every_cluster = lax.all_gather(merged, "client", axis=1, tiled=True)
    result = lax.dynamic_index_in_dim(every_cluster, own_cluster, 0, keepdims=True)
    return result


def solution(mesh):
    placed = (
        P("client", None, None, "mp"),
        P("client", "mp", None),
        P("client", None, "mp", None),
        P("client", None, "mp"),
        P("client", None, "mp", None),
        P(),
    )
    return jax.shard_map(
        body, mesh=mesh, in_specs=placed, out_specs=P("client", "mp", None), check_vma=False
    )
```

profile of v0, /device:TPU:1, one launch (start us, length us, event | category | flops | bytes accessed | tf_op | source)
XLA Modules:
  0.0 917.2 jit_solution(14706498457414140986)
XLA Ops:
  18.3 7.8 copy.31
  26.7 23.7 %reduce.10 = bf16[896,2048]{1,0:T(8,128)(2,1)} reduce(bf16[896,1,2048]{2,1,0:T(2,128)(2,1)} %bitcast.73, bf16[]{:T(256)} %broadcast.41), dimensions={1}, to_apply=%bitcast.72.reduce_sub_computation | reduce | bytes 7340034
  50.3 8.7 reshape.64
  59.1 10.4 %all-to-all-start.1 = ((bf16[32,2,28672]{2,1,0:T(2,128)(2,1)}), bf16[32,2,28672]{2,1,0:T(2,128)(2,1)}, u32[]{:S(2)}, u32[]{:S(2)}) async-start(bf16[32,2,28672]{2,1,0:T(2,128)(2,1)} %reshape.64), calls=%async_computation.5 | async-start | bytes 7340032 | tf_op jit(solution)/shard_map/all_to_all | solution.py:43
  73.3 27.6 %reduce-scatter.11.cloned.1.call-done = f32[16,2048]{1,0:T(8,128)} async-done(((f32[128,2048]{1,0:T(8,128)}), f32[16,2048]{1,0:T(8,128)}) %reduce-scatter.11.cloned.1.call-update) | async-done | bytes 131088 | tf_op jit(solution)/shard_map/reduce_scatter | solution.py:19
  100.9 95.0 %reduce-scatter.5.cloned.1.call-done = f32[16,2048]{1,0:T(8,128)} async-done(((f32[128,2048]{1,0:T(8,128)}), f32[16,2048]{1,0:T(8,128)}) %reduce-scatter.5.cloned.1.call-update) | async-done | bytes 131088 | tf_op jit(solution)/shard_map/reduce_scatter | solution.py:19
  195.9 86.6 %reduce-scatter.7.cloned.1.call-done = f32[16,2048]{1,0:T(8,128)} async-done(((f32[128,2048]{1,0:T(8,128)}), f32[16,2048]{1,0:T(8,128)}) %reduce-scatter.7.cloned.1.call-update) | async-done | bytes 131088 | tf_op jit(solution)/shard_map/reduce_scatter | solution.py:19
  282.5 87.1 %reduce-scatter.9.cloned.1.call-done = f32[16,2048]{1,0:T(8,128)} async-done(((f32[128,2048]{1,0:T(8,128)}), f32[16,2048]{1,0:T(8,128)}) %reduce-scatter.9.cloned.1.call-update) | async-done | bytes 131088 | tf_op jit(solution)/shard_map/reduce_scatter | solution.py:19
  370.9 41.3 %all_gather.17 = bf16[128,2048]{1,0:T(8,128)(2,1)S(1)} all-gather(bf16[16,2048]{1,0:T(8,128)(2,1)S(1)} %get-tuple-element.12), channel_id=1, replica_groups=mesh['client'=32,'mp'=8] {'mp'}, dimensions={0}, use_global_device_ids=true | all-gather | bytes 589824 | tf_op jit(solution)/shard_map/all_gather | solution.py:33
  412.1 42.5 %all_gather.16 = bf16[128,2048]{1,0:T(8,128)(2,1)S(1)} all-gather(bf16[16,2048]{1,0:T(8,128)(2,1)S(1)} %get-tuple-element.10), channel_id=1, replica_groups=mesh['client'=32,'mp'=8] {'mp'}, dimensions={0}, use_global_device_ids=true | all-gather | bytes 589824 | tf_op jit(solution)/shard_map/all_gather | solution.py:33
  454.6 42.9 %all_gather.15 = bf16[128,2048]{1,0:T(8,128)(2,1)S(1)} all-gather(bf16[16,2048]{1,0:T(8,128)(2,1)S(1)} %get-tuple-element.11), channel_id=1, replica_groups=mesh['client'=32,'mp'=8] {'mp'}, dimensions={0}, use_global_device_ids=true | all-gather | bytes 589824 | tf_op jit(solution)/shard_map/all_gather | solution.py:33
  497.5 41.5 %all_gather.18 = bf16[128,2048]{1,0:T(8,128)(2,1)S(1)} all-gather(bf16[16,2048]{1,0:T(8,128)(2,1)S(1)} %get-tuple-element.9), channel_id=1, replica_groups=mesh['client'=32,'mp'=8] {'mp'}, dimensions={0}, use_global_device_ids=true | all-gather | bytes 589824 | tf_op jit(solution)/shard_map/all_gather | solution.py:33
  542.5 4.9 fusion.51
  547.3 21.0 %psum.7 = f32[]{:T(128)} all-reduce(f32[]{:T(128)} %get-tuple-element.17), channel_id=1, replica_groups=mesh['client'=32,'mp'=8] {'mp'}, use_global_device_ids=true, to_apply=%region_9.10 | all-reduce | flops 1 | bytes 8 | tf_op jit(solution)/shard_map/psum | solution.py:38
  569.0 5.7 fusion.12
  574.7 18.1 %copy.15 = bf16[1,896,2048]{2,0,1:T(2,128)(2,1)} copy(bf16[1,896,2048]{1,2,0:T(8,128)(2,1)} %fusion.12) | data formatting | bytes 7340032 | tf_op jit(solution)/shard_map/broadcast_in_dim | solution.py:42
  592.8 23.7 %reduce.9 = bf16[896,2048]{1,0:T(8,128)(2,1)} reduce(bf16[896,1,2048]{2,1,0:T(2,128)(2,1)} %bitcast.74, bf16[]{:T(256)} %broadcast.41), dimensions={1}, to_apply=%bitcast.59.reduce_sub_computation | reduce | bytes 7340034
  616.5 8.7 reshape.62
  625.2 38.2 %all-to-all-start = ((bf16[32,2,28672]{2,1,0:T(2,128)(2,1)}), bf16[32,2,28672]{2,1,0:T(2,128)(2,1)}, u32[]{:S(2)}, u32[]{:S(2)}) async-start(bf16[32,2,28672]{2,1,0:T(2,128)(2,1)} %reshape.62), calls=%async_computation.4 | async-start | bytes 7340032 | tf_op jit(solution)/shard_map/all_to_all | solution.py:42
  663.4 19.3 %reshape.65 = bf16[896,1,2048]{2,1,0:T(2,128)(2,1)} reshape(bf16[32,2,28672]{2,1,0:T(2,128)(2,1)} %all-to-all-done.1) | data formatting | bytes 7340032
  682.7 24.4 %convert_reduce_fusion = f32[896,2048]{1,0:T(8,128)} fusion(bf16[896,1,2048]{2,1,0:T(2,128)(2,1)} %reshape.65), kind=kLoop, calls=%fused_computation.4 | loop fusion | flops 1835008 | bytes 11010048 | tf_op jit(solution)/shard_map/convert_element_type | solution.py:47
  707.1 8.0 reshape.58
  715.1 30.2 %all-to-all-done = bf16[32,2,28672]{2,1,0:T(2,128)(2,1)} async-done(((bf16[32,2,28672]{2,1,0:T(2,128)(2,1)}), bf16[32,2,28672]{2,1,0:T(2,128)(2,1)}, u32[]{:S(2)}, u32[]{:S(2)}) %all-to-all-start) | async-done | bytes 3670048 | tf_op jit(solution)/shard_map/all_to_all | solution.py:42
  745.3 19.3 %reshape.63 = bf16[896,1,2048]{2,1,0:T(2,128)(2,1)} reshape(bf16[32,2,28672]{2,1,0:T(2,128)(2,1)} %all-to-all-done) | data formatting | bytes 7340032
  764.6 23.6 %bitcast_reduce_fusion = bf16[896,2048]{1,0:T(8,128)(2,1)} fusion(bf16[896,1,2048]{2,1,0:T(2,128)(2,1)} %reshape.63), kind=kLoop, calls=%fused_computation.65 | loop fusion | bytes 7340032 | tf_op jit(solution)/shard_map/all_to_all | solution.py:42
  788.2 5.9 all_to_all.7
  794.1 6.0 convert_multiply_fusion
  800.2 4.0 fusion.10
  804.2 7.7 fusion.16
  814.5 82.3 %all-gather.2.cloned.1.call-done = bf16[4,896,2048]{2,0,1:T(4,128)(2,1)} async-done(((bf16[4,28,2048]{2,0,1:T(4,128)(2,1)}), bf16[4,896,2048]{2,0,1:T(4,128)(2,1)}) %all-gather.2.cloned.1.call-update) | async-done | bytes 14680080 | tf_op jit(solution)/shard_map/all_gather | solution.py:54
  896.8 9.3 %constant_dynamic-slice_fusion = bf16[1,896,2048]{2,0,1:T(2,128)(2,1)S(1)} fusion(bf16[4,896,2048]{2,0,1:T(4,128)(2,1)} %all-gather.2.cloned.1.call-done, s32[]{:T(128)S(6)} %select_n.42), kind=kLoop, calls=%fused_computation.62 | loop fusion | bytes 7340036 | tf_op jit(solution)/shard_map/jit(dynamic_index_in_dim)/dynamic_slice | solution.py:55
  906.1 4.1 copy.19
  (35 shorter events, 21.5 us)
Async XLA Ops:
  6.5 8.0 copy-start.1
  6.5 94.4 %reduce-scatter.11.cloned.1.call-start = ((), (), s32[]{:S(2)}) async-start(), calls=%async_computation.9 | async-start | bytes 1179648 | tf_op jit(solution)/shard_map/reduce_scatter | solution.py:19
  10.5 185.4 %reduce-scatter.5.cloned.1.call-start = ((), (), s32[]{:S(2)}) async-start(), calls=%async_computation.6 | async-start | bytes 1179648 | tf_op jit(solution)/shard_map/reduce_scatter | solution.py:19
  14.5 268.1 %reduce-scatter.7.cloned.1.call-start = ((), (), s32[]{:S(2)}) async-start(), calls=%async_computation.7 | async-start | bytes 1179648 | tf_op jit(solution)/shard_map/reduce_scatter | solution.py:19
  59.1 14.2 %copy-start.3 = (s32[1,4,16,2]{2,3,1,0:T(2,128)S(1)}, s32[1,4,16,2]{2,3,1,0:T(2,128)}, u32[]{:S(2)}) copy-start(s32[1,4,16,2]{2,3,1,0:T(2,128)} %param.10) | copy-start | bytes 1540
  59.1 14.2 %copy-start.5 = (f32[1,4,16]{2,1,0:T(4,128)S(1)}, f32[1,4,16]{2,1,0:T(4,128)}, u32[]{:S(2)}) copy-start(f32[1,4,16]{2,1,0:T(4,128)} %param.9) | copy-start | bytes 772
  59.1 310.6 %copy-start.2 = (bf16[1,4,16,2048]{3,2,1,0:T(8,128)(2,1)S(1)}, bf16[1,4,16,2048]{3,2,1,0:T(8,128)(2,1)}, u32[]{:S(2)}) copy-start(bf16[1,4,16,2048]{3,2,1,0:T(8,128)(2,1)} %param.8) | copy-start | bytes 786436
  59.1 566.1 %all-to-all-start.1 = ((bf16[32,2,28672]{2,1,0:T(2,128)(2,1)}), bf16[32,2,28672]{2,1,0:T(2,128)(2,1)}, u32[]{:S(2)}, u32[]{:S(2)}) async-start(bf16[32,2,28672]{2,1,0:T(2,128)(2,1)} %reshape.64), calls=%async_computation.5 | async-start | bytes 7340032 | tf_op jit(solution)/shard_map/all_to_all | solution.py:43
  69.4 300.2 %reduce-scatter.9.cloned.1.call-start = ((), (), s32[]{:S(2)}) async-start(), calls=%async_computation.8 | async-start | bytes 1179648 | tf_op jit(solution)/shard_map/reduce_scatter | solution.py:19
  625.2 120.1 %all-to-all-start = ((bf16[32,2,28672]{2,1,0:T(2,128)(2,1)}), bf16[32,2,28672]{2,1,0:T(2,128)(2,1)}, u32[]{:S(2)}, u32[]{:S(2)}) async-start(bf16[32,2,28672]{2,1,0:T(2,128)(2,1)} %reshape.62), calls=%async_computation.4 | async-start | bytes 7340032 | tf_op jit(solution)/shard_map/all_to_all | solution.py:42
  663.4 233.5 %all-gather.2.cloned.1.call-start = ((), (), s32[]{:S(2)}) async-start(), calls=%async_computation.10 | async-start | bytes 15138816 | tf_op jit(solution)/shard_map/all_gather | solution.py:54
  794.1 6.0 copy-start
  794.1 6.0 copy-start.4
Sparse Core Ops, SparseCore 0:
  11.3 89.5 reduce-scatter.10
  105.3 90.5 reduce-scatter.4
  199.8 82.6 reduce-scatter.6
  286.8 82.7 reduce-scatter.8
  812.1 84.7 all-gather.1
where the time goes:
time: 926 us; the launch traced here: 917 us
  waiting for transfers between devices  409 us (44%)
  blocking collectives  189 us (20%)
  local copies, waits for them, and re-layouts  134 us (14%)
  other arithmetic  84.6 us (9%)
  starting transfers between devices  48.7 us (5%)
  matrix products  35.4 us (4%)
  between operations  16.3 us (2%)
    reduce_scatter x4, waiting for transfers between devices, body(): lax.psum_scatter(jnp.dot(batch_hidden, local_weight, preferred_element_ty...  296 us
    all_gather x4, blocking collectives, body(): lax.all_gather(grad_out, 'mp', axis=0, tiled=True)  168 us
    all_gather x1, waiting for transfers between devices, body(): every_cluster = lax.all_gather(merged, 'client', axis=1, tiled=True)  82.3 us
    unnamed x18, local copies, waits for them, and re-layouts  64.4 us
    unnamed x2, other arithmetic  47.4 us
    all_to_all x1, starting transfers between devices, body(): lax.all_to_all(a_weight[None], 'client', split_axis=1, concat_axis=0, til...  38.2 us
    all_to_all x1, waiting for transfers between devices, body(): lax.all_to_all(a_weight[None], 'client', split_axis=1, concat_axis=0, til...  30.2 us
    all_to_all x2, local copies, waits for them, and re-layouts, body(): lax.all_to_all(a_weight[None], 'client', split_axis=1, concat_axis=0, til...  29.5 us
  transfers between devices with their start and end apart: 7, of which 6 were waited for; matrix products, arithmetic and copies ran while one was open for 19% of the time, Pallas kernels for 0%

commit v1 on v0

--- a/solution.py
+++ b/solution.py
@@ -51,7 +51,9 @@
     own_cluster = lax.dynamic_index_in_dim(
         assign[:, 0], lax.axis_index("client"), 0, keepdims=False
     )
-    every_cluster = lax.all_gather(merged, "client", axis=1, tiled=True)
+    every_cluster = jnp.concatenate(
+        lax.all_to_all(jnp.stack([merged] * lax.axis_size("client")), "client", 0, 0), axis=1
+    )
     result = lax.dynamic_index_in_dim(every_cluster, own_cluster, 0, keepdims=True)
     return result
 

time: 926 us -> 1180 us (1.27)
  waiting for transfers between devices: 409 us -> 650 us
    all_to_all x0 -> x1, waiting for transfers between devices: none -> 324 us  [body(): lax.all_to_all(jnp.stack([merged] * lax.axis_size('client')), 'client', 0...]
    all_gather x1 -> x0, waiting for transfers between devices: 82.3 us -> none  [body(): every_cluster = lax.all_gather(merged, 'client', axis=1, tiled=True)]
  transfers between devices with their start and end apart: 7 -> 7, of which waited for: 6 -> 6; matrix products, arithmetic and copies ran while one was open for 19% -> 15% of each run, Pallas kernels for 0% -> 0%
where the time goes in v1:
time: 1180 us; the launch traced here: 1170 us
  waiting for transfers between devices  650 us (55%)
  blocking collectives  189 us (16%)
  local copies, waits for them, and re-layouts  142 us (12%)
  other arithmetic  84.6 us (7%)
  starting transfers between devices  55.3 us (5%)
  matrix products  34.6 us (3%)
  between operations  16.3 us (1%)
    all_to_all x1, waiting for transfers between devices, body(): lax.all_to_all(jnp.stack([merged] * lax.axis_size('client')), 'client', 0...  324 us
    reduce_scatter x4, waiting for transfers between devices, body(): lax.psum_scatter(jnp.dot(batch_hidden, local_weight, preferred_element_ty...  296 us
    all_gather x4, blocking collectives, body(): lax.all_gather(grad_out, 'mp', axis=0, tiled=True)  168 us
    unnamed x18, local copies, waits for them, and re-layouts  64.4 us
    unnamed x2, other arithmetic  47.4 us
    all_to_all x1, starting transfers between devices, body(): lax.all_to_all(a_weight[None], 'client', split_axis=1, concat_axis=0, til...  38.2 us
    all_to_all x1, waiting for transfers between devices, body(): lax.all_to_all(a_weight[None], 'client', split_axis=1, concat_axis=0, til...  30.2 us
    all_to_all x2, local copies, waits for them, and re-layouts, body(): lax.all_to_all(a_weight[None], 'client', split_axis=1, concat_axis=0, til...  29.5 us
  transfers between devices with their start and end apart: 7, of which 6 were waited for; matrix products, arithmetic and copies ran while one was open for 15% of the time, Pallas kernels for 0%

profile of v1, /device:TPU:1, one launch (start us, length us, event | category | flops | bytes accessed | tf_op | source)
XLA Modules:
  0.0 1172.5 jit_solution(10727283459516548430)
XLA Ops:
  18.3 7.8 copy.31
  26.7 23.7 %reduce.10 = bf16[896,2048]{1,0:T(8,128)(2,1)} reduce(bf16[896,1,2048]{2,1,0:T(2,128)(2,1)} %bitcast.76, bf16[]{:T(256)} %broadcast.43), dimensions={1}, to_apply=%bitcast.75.reduce_sub_computation | reduce | bytes 7340034
  50.3 8.7 reshape.74
  59.1 10.4 all-to-all-start.1
  73.3 27.6 %reduce-scatter.11.cloned.1.call-done = f32[16,2048]{1,0:T(8,128)} async-done(((f32[128,2048]{1,0:T(8,128)}), f32[16,2048]{1,0:T(8,128)}) %reduce-scatter.11.cloned.1.call-update) | async-done | bytes 131088 | tf_op jit(solution)/shard_map/reduce_scatter | solution.py:19
  100.9 95.0 %reduce-scatter.5.cloned.1.call-done = f32[16,2048]{1,0:T(8,128)} async-done(((f32[128,2048]{1,0:T(8,128)}), f32[16,2048]{1,0:T(8,128)}) %reduce-scatter.5.cloned.1.call-update) | async-done | bytes 131088 | tf_op jit(solution)/shard_map/reduce_scatter | solution.py:19
  195.9 86.6 %reduce-scatter.7.cloned.1.call-done = f32[16,2048]{1,0:T(8,128)} async-done(((f32[128,2048]{1,0:T(8,128)}), f32[16,2048]{1,0:T(8,128)}) %reduce-scatter.7.cloned.1.call-update) | async-done | bytes 131088 | tf_op jit(solution)/shard_map/reduce_scatter | solution.py:19
  282.5 87.1 %reduce-scatter.9.cloned.1.call-done = f32[16,2048]{1,0:T(8,128)} async-done(((f32[128,2048]{1,0:T(8,128)}), f32[16,2048]{1,0:T(8,128)}) %reduce-scatter.9.cloned.1.call-update) | async-done | bytes 131088 | tf_op jit(solution)/shard_map/reduce_scatter | solution.py:19
  370.9 41.3 %all_gather.14 = bf16[128,2048]{1,0:T(8,128)(2,1)S(1)} all-gather(bf16[16,2048]{1,0:T(8,128)(2,1)S(1)} %get-tuple-element.12), channel_id=1, replica_groups=mesh['client'=32,'mp'=8] {'mp'}, dimensions={0}, use_global_device_ids=true | all-gather | bytes 589824 | tf_op jit(solution)/shard_map/all_gather | solution.py:33
  412.1 42.5 %all_gather.13 = bf16[128,2048]{1,0:T(8,128)(2,1)S(1)} all-gather(bf16[16,2048]{1,0:T(8,128)(2,1)S(1)} %get-tuple-element.10), channel_id=1, replica_groups=mesh['client'=32,'mp'=8] {'mp'}, dimensions={0}, use_global_device_ids=true | all-gather | bytes 589824 | tf_op jit(solution)/shard_map/all_gather | solution.py:33
  454.6 42.9 %all_gather.12 = bf16[128,2048]{1,0:T(8,128)(2,1)S(1)} all-gather(bf16[16,2048]{1,0:T(8,128)(2,1)S(1)} %get-tuple-element.11), channel_id=1, replica_groups=mesh['client'=32,'mp'=8] {'mp'}, dimensions={0}, use_global_device_ids=true | all-gather | bytes 589824 | tf_op jit(solution)/shard_map/all_gather | solution.py:33
  497.5 41.5 %all_gather.15 = bf16[128,2048]{1,0:T(8,128)(2,1)S(1)} all-gather(bf16[16,2048]{1,0:T(8,128)(2,1)S(1)} %get-tuple-element.9), channel_id=1, replica_groups=mesh['client'=32,'mp'=8] {'mp'}, dimensions={0}, use_global_device_ids=true | all-gather | bytes 589824 | tf_op jit(solution)/shard_map/all_gather | solution.py:33
  542.5 4.9 fusion.51
  547.3 21.0 %psum.7 = f32[]{:T(128)} all-reduce(f32[]{:T(128)} %get-tuple-element.17), channel_id=1, replica_groups=mesh['client'=32,'mp'=8] {'mp'}, use_global_device_ids=true, to_apply=%region_9.10 | all-reduce | flops 1 | bytes 8 | tf_op jit(solution)/shard_map/psum | solution.py:38
  569.0 5.7 fusion.12
  574.7 18.1 %copy.15 = bf16[1,896,2048]{2,0,1:T(2,128)(2,1)} copy(bf16[1,896,2048]{1,2,0:T(8,128)(2,1)} %fusion.12) | data formatting | bytes 7340032 | tf_op jit(solution)/shard_map/broadcast_in_dim | solution.py:42
  592.8 23.7 %reduce.9 = bf16[896,2048]{1,0:T(8,128)(2,1)} reduce(bf16[896,1,2048]{2,1,0:T(2,128)(2,1)} %bitcast.77, bf16[]{:T(256)} %broadcast.43), dimensions={1}, to_apply=%bitcast.62.reduce_sub_computation | reduce | bytes 7340034
  616.5 8.7 reshape.72
  625.2 38.2 %all-to-all-start = ((bf16[32,2,28672]{2,1,0:T(2,128)(2,1)}), bf16[32,2,28672]{2,1,0:T(2,128)(2,1)}, u32[]{:S(2)}, u32[]{:S(2)}) async-start(bf16[32,2,28672]{2,1,0:T(2,128)(2,1)} %reshape.72), calls=%async_computation.4 | async-start | bytes 7340032 | tf_op jit(solution)/shard_map/all_to_all | solution.py:42
  663.4 19.3 %reshape.75 = bf16[896,1,2048]{2,1,0:T(2,128)(2,1)} reshape(bf16[32,2,28672]{2,1,0:T(2,128)(2,1)} %all-to-all-done.1) | data formatting | bytes 7340032
  682.7 24.4 %convert_reduce_fusion = f32[896,2048]{1,0:T(8,128)} fusion(bf16[896,1,2048]{2,1,0:T(2,128)(2,1)} %reshape.75), kind=kLoop, calls=%fused_computation.4 | loop fusion | flops 1835008 | bytes 11010048 | tf_op jit(solution)/shard_map/convert_element_type | solution.py:47
  707.1 8.0 reshape.68
  715.1 30.2 %all-to-all-done = bf16[32,2,28672]{2,1,0:T(2,128)(2,1)} async-done(((bf16[32,2,28672]{2,1,0:T(2,128)(2,1)}), bf16[32,2,28672]{2,1,0:T(2,128)(2,1)}, u32[]{:S(2)}, u32[]{:S(2)}) %all-to-all-start) | async-done | bytes 3670048 | tf_op jit(solution)/shard_map/all_to_all | solution.py:42
  745.3 19.3 %reshape.73 = bf16[896,1,2048]{2,1,0:T(2,128)(2,1)} reshape(bf16[32,2,28672]{2,1,0:T(2,128)(2,1)} %all-to-all-done) | data formatting | bytes 7340032
  764.6 23.6 %bitcast_reduce_fusion = bf16[896,2048]{1,0:T(8,128)(2,1)} fusion(bf16[896,1,2048]{2,1,0:T(2,128)(2,1)} %reshape.73), kind=kLoop, calls=%fused_computation.65 | loop fusion | bytes 7340032 | tf_op jit(solution)/shard_map/all_to_all | solution.py:42
  788.2 5.9 all_to_all.9
  794.1 6.0 convert_multiply_fusion
  804.2 7.0 fusion.16
  811.1 8.3 stack.2
  819.5 6.6 all-to-all-start.2
  828.6 323.5 %all-to-all-done.2 = bf16[32,4,28,2048]{3,1,2,0:T(4,128)(2,1)} async-done(((bf16[32,4,28,2048]{3,1,2,0:T(4,128)(2,1)}), bf16[32,4,28,2048]{3,1,2,0:T(4,128)(2,1)}, u32[]{:S(2)}, u32[]{:S(2)}) %all-to-all-start.2) | async-done | bytes 14680096 | tf_op jit(solution)/shard_map/all_to_all | solution.py:55
  1152.1 9.3 constant_dynamic-slice_fusion
  (35 shorter events, 29.5 us)
Async XLA Ops:
  6.5 8.0 copy-start.1
  6.5 94.4 %reduce-scatter.11.cloned.1.call-start = ((), (), s32[]{:S(2)}) async-start(), calls=%async_computation.10 | async-start | bytes 1179648 | tf_op jit(solution)/shard_map/reduce_scatter | solution.py:19
  10.5 185.4 %reduce-scatter.5.cloned.1.call-start = ((), (), s32[]{:S(2)}) async-start(), calls=%async_computation.7 | async-start | bytes 1179648 | tf_op jit(solution)/shard_map/reduce_scatter | solution.py:19
  14.5 268.1 %reduce-scatter.7.cloned.1.call-start = ((), (), s32[]{:S(2)}) async-start(), calls=%async_computation.8 | async-start | bytes 1179648 | tf_op jit(solution)/shard_map/reduce_scatter | solution.py:19
  59.1 14.2 %copy-start.3 = (s32[1,4,16,2]{2,3,1,0:T(2,128)S(1)}, s32[1,4,16,2]{2,3,1,0:T(2,128)}, u32[]{:S(2)}) copy-start(s32[1,4,16,2]{2,3,1,0:T(2,128)} %param.10) | copy-start | bytes 1540
  59.1 14.2 %copy-start.5 = (f32[1,4,16]{2,1,0:T(4,128)S(1)}, f32[1,4,16]{2,1,0:T(4,128)}, u32[]{:S(2)}) copy-start(f32[1,4,16]{2,1,0:T(4,128)} %param.9) | copy-start | bytes 772
  59.1 310.6 %copy-start.2 = (bf16[1,4,16,2048]{3,2,1,0:T(8,128)(2,1)S(1)}, bf16[1,4,16,2048]{3,2,1,0:T(8,128)(2,1)}, u32[]{:S(2)}) copy-start(bf16[1,4,16,2048]{3,2,1,0:T(8,128)(2,1)} %param.8) | copy-start | bytes 786436
  59.1 566.1 %all-to-all-start.1 = ((bf16[32,2,28672]{2,1,0:T(2,128)(2,1)}), bf16[32,2,28672]{2,1,0:T(2,128)(2,1)}, u32[]{:S(2)}, u32[]{:S(2)}) async-start(bf16[32,2,28672]{2,1,0:T(2,128)(2,1)} %reshape.74), calls=%async_computation.5 | async-start | bytes 7340032 | tf_op jit(solution)/shard_map/all_to_all | solution.py:43
  69.4 300.2 %reduce-scatter.9.cloned.1.call-start = ((), (), s32[]{:S(2)}) async-start(), calls=%async_computation.9 | async-start | bytes 1179648 | tf_op jit(solution)/shard_map/reduce_scatter | solution.py:19
  625.2 120.1 %all-to-all-start = ((bf16[32,2,28672]{2,1,0:T(2,128)(2,1)}), bf16[32,2,28672]{2,1,0:T(2,128)(2,1)}, u32[]{:S(2)}, u32[]{:S(2)}) async-start(bf16[32,2,28672]{2,1,0:T(2,128)(2,1)} %reshape.72), calls=%async_computation.4 | async-start | bytes 7340032 | tf_op jit(solution)/shard_map/all_to_all | solution.py:42
  794.1 6.0 copy-start
  794.1 6.0 copy-start.4
  819.5 332.7 %all-to-all-start.2 = ((bf16[32,4,28,2048]{3,1,2,0:T(4,128)(2,1)}), bf16[32,4,28,2048]{3,1,2,0:T(4,128)(2,1)}, u32[]{:S(2)}, u32[]{:S(2)}) async-start(bf16[32,4,28,2048]{3,1,2,0:T(4,128)(2,1)} %stack.2), calls=%async_computation.6 | async-start | bytes 29360128 | tf_op jit(solution)/shard_map/all_to_all | solution.py:55
Sparse Core Ops, SparseCore 0:
  11.3 89.5 reduce-scatter.10
  105.3 90.5 reduce-scatter.4
  199.8 82.6 reduce-scatter.6
  286.8 82.7 reduce-scatter.8
